TPU v7x, 32 devices: a whole 2x2x4 slice. The times are simulated.
32 devices in a mesh: pb: 4 (over z), row: 4 (over y, x), col: 2 (over core).
Axes of the slice: x: 2, y: 2, z: 4, core: 2. Of those that a mesh axis runs over, the one named last changes fastest.
Arguments:
- amplitudes: bfloat16 [4, 20, 4, 9216], P('pb'), may hold values from -6 to 6
- pairs: int32 [4, 4, 2], P('pb'), may hold values from 0 to 3
- stored_k: int32 [4], replicated, may hold values from 0 to 3, each once
- orbitals: bfloat16 [4, 192, 2048], P('pb', None, ('row', 'col')), may hold values from -1.078125 to 1.078125
- valence_energy: float32 [4, 96], replicated, may hold values from -1 to 0
- conduction_energy: float32 [4, 96], replicated, may hold values from 2.5 to 3.5
- screened: bfloat16 [4, 2048, 2048], P('pb', 'row', 'col'), may hold values from -0.125 to 0.125
Outputs:
- filtered: bfloat16 [4, 20, 4, 9216], P('pb')
Inputs may be any that keep to these rules, and one draw needn't show every extreme that they name: stored_k holds every k-point exactly once; row s of orbitals belongs to k-point stored_k[s]. `pairs`: each entry is a k-point.
All inputs are finite; a program needn't handle non-finite values.
Results may differ from a plain program's by a relative error of at most 0.024.
Values may be sent and summed in bfloat16 or wider, within the bound.
A program may use at most 64 MiB of HBM per device.

v0:
```python
import jax
import jax.numpy as jnp
from jax import lax
from jax.sharding import PartitionSpec as P

CENTER = 3.0
HALF = 2.5


def on_device(amplitudes, pairs, stored_k, orbitals, valence_energy, conduction_energy, screened):
    amplitude = amplitudes[0]
    pair_list = pairs[0]
    w_tile = screened[0]
    count_v = valence_energy.shape[1]
    count_c = conduction_energy.shape[1]
    vectors, pair_count, flat_size = amplitude.shape
    points = orbitals.shape[2]
    col_width = w_tile.shape[1]
    column = lax.axis_index("col")

    def pick(shard_piece):
        pick_low = (stored_k[None, :] == pair_list[:, 0:1]).astype(jnp.bfloat16)
        pick_high = (stored_k[None, :] == pair_list[:, 1:2]).astype(jnp.bfloat16)
        low_bands = jnp.einsum(
            "pl,lbr->pbr", pick_low, shard_piece[:, :count_v], preferred_element_type=jnp.float32
        )
        high_bands = jnp.einsum(
            "pl,lbr->pbr", pick_high, shard_piece[:, count_v:], preferred_element_type=jnp.float32
        )
        return (low_bands, high_bands)

    def fetch_each():
        found = pick(lax.all_gather(orbitals, "pb", axis=0, tiled=True))
        return (found[0].astype(jnp.bfloat16), found[1].astype(jnp.bfloat16))

    low_energy = jnp.take(valence_energy, pair_list[:, 0], axis=0)
    high_energy = jnp.take(conduction_energy, pair_list[:, 1], axis=0)
    gap_grid = (high_energy[:, None, :] - low_energy[:, :, None]).reshape(pair_count, flat_size)
    gap_rows = jnp.tile(gap_grid, (vectors, 1))

    def kernel_term(current, bands):
        valence, conduction_orbital = bands
        amplitude_lattice = current.reshape(vectors, pair_count, count_v, count_c)
        inner_total_sum = jnp.einsum(
            "iomx,oxj->iomj",
            amplitude_lattice,
            conduction_orbital,
            preferred_element_type=jnp.float32,
        )
        values = jnp.sum(valence.astype(jnp.float32)[None] * inner_total_sum, axis=2)
        values = values.astype(jnp.bfloat16).reshape(vectors * pair_count, points)
        everywhere = lax.all_gather(values, ("row", "col"), axis=1, tiled=True)
        needed = lax.dynamic_slice_in_dim(everywhere, column * col_width, col_width, 1)
        partial_value = lax.dot_general(
            needed, w_tile, (((1,), (1,)), ((), ())), preferred_element_type=jnp.float32
        )
        own_sums = (
            lax.psum_scatter(
                partial_value.astype(jnp.bfloat16), "col", scatter_dimension=1, tiled=True
            )
            .astype(jnp.float32)
            .reshape(vectors, pair_count, points)
        )
        weighted_product = (valence.astype(jnp.float32)[None] * own_sums[:, :, None, :]).astype(
            jnp.bfloat16
        )
        projected = jnp.einsum(
            "kyqz,yhz->kyqh",
            weighted_product,
            conduction_orbital,
            preferred_element_type=jnp.float32,
        )
        return projected.reshape(vectors * pair_count, flat_size)

    def advance(current_rows, summed, gap_part, previous_rows, factor):
        value = (gap_part * current_rows + summed - CENTER * current_rows) / HALF
        if previous_rows is None:
            return value.astype(jnp.bfloat16)
        return (factor * value - previous_rows).astype(jnp.bfloat16)

    def finish(partial_term, current, previous, factor):
        summed = lax.psum(partial_term.astype(jnp.bfloat16), ("row", "col")).astype(jnp.float32)
        previous_full = None
        if previous is not None:
            previous_full = previous.astype(jnp.float32)
        return advance(current.astype(jnp.float32), summed, gap_rows, previous_full, factor)

    initial = amplitude.reshape(vectors * pair_count, flat_size)
    first_bands = fetch_each()
    first_term = finish(kernel_term(initial, first_bands), initial, None, 1.0)
    second_bands = fetch_each()
    second_term = finish(kernel_term(first_term, second_bands), first_term, initial, 2.0)
    return second_term.reshape(1, vectors, pair_count, flat_size)


def solution(mesh):
    return jax.shard_map(
        on_device,
        mesh=mesh,
        in_specs=(
            P("pb", None, None, None),
            P("pb", None, None),
            P(),
            P("pb", None, ("row", "col")),
            P(),
            P(),
            P("pb", "row", "col"),
        ),
        out_specs=P("pb", None, None, None),
        check_vma=False,
    )
```

profile of v0, /device:TPU:0, one launch (start us, length us, event | category | flops | bytes accessed | tf_op | source)
XLA Modules:
  0.0 231.6 jit_solution(977043757335007725)
XLA Ops:
  6.5 0.8 slice_bitcast_fusion.1
  7.4 16.6 %all_gather.10 = bf16[4,192,256]{2,1,0:T(8,128)(2,1)S(1)} all-gather(bf16[1,192,256]{2,1,0:T(8,128)(2,1)} %param.12), channel_id=1, replica_groups=mesh['pb'=4,'row'=4,'col'=2] {'pb'}, dimensions={0}, use_global_device_ids=true | all-gather | bytes 491520 | tf_op jit(solution)/shard_map/all_gather | solution.py:33
  24.0 1.0 fusion.15
  25.0 0.1 copy.59
  25.1 0.0 copy-done.1
  25.1 2.6 %reshape_reshape_squeeze.3 = bf16[20,4,96,96]{3,2,1,0:T(8,128)(2,1)} reshape(bf16[1,20,4,9216]{3,2,1,0:T(4,128)(2,1)S(1)} %copy-done.1) | data formatting | bytes 2949120 | tf_op jit(solution)/shard_map/reshape;reshape;squeeze | solution.py:43
  27.7 0.0 copy-done.5
  27.7 0.3 fusion.16
  28.0 2.8 %fusion.1 = bf16[20,4,256]{2,0,1:T(8,128)(2,1)S(1)} fusion(f32[4,96,256]{2,1,0:T(8,128)S(1)} %copy.59, bf16[20,4,96,96]{3,2,1,0:T(8,128)(2,1)} %reshape_reshape_squeeze.3, bf16[4,96,256,1]{2,0,1,3:T(4,128)(2,1)S(1)} %fusion.16), kind=kOutput, calls=%fused_computation.5 | convolution fusion | flops 381399040 | bytes 2105344 | tf_op jit(solution)/shard_map/iomx,oxj->iomj/dot_general | solution.py:44
  30.9 10.1 %all_gather.11 = bf16[80,2048]{1,0:T(8,128)(2,1)S(1)} all-gather(bf16[80,256]{1,0:T(8,128)(2,1)S(1)} %convert_element_type.92), channel_id=1, replica_groups=mesh['pb'=4,'row'=4,'col'=2] {'row','col'}, dimensions={1}, use_global_device_ids=true | all-gather | bytes 368640 | tf_op jit(solution)/shard_map/all_gather | solution.py:52
  41.0 1.1 convolution_convert_fusion.3
  42.1 0.0 reduce-scatter.3.cloned.1.call-update
  42.1 0.0 all-reduce.3.cloned.1.call-start
  42.2 1.7 reshape.48
  43.9 6.7 %reduce-scatter.3.cloned.1.call-done = bf16[80,256]{1,0:T(8,128)(2,1)} async-done(((bf16[80,512]{1,0:T(8,128)(2,1)}), bf16[80,256]{1,0:T(8,128)(2,1)}) %reduce-scatter.3.cloned.1.call-update) | async-done | bytes 40976 | tf_op jit(solution)/shard_map/reduce_scatter | solution.py:58
  50.6 0.8 reshape.49
  51.4 2.9 %convert_bitcast_fusion.1 = bf16[20,4,96,96]{2,3,0,1:T(8,128)(2,1)} fusion(f32[20,4,256]{2,0,1:T(8,128)S(1)} %copy.63, f32[4,96,256]{2,1,0:T(8,128)S(1)} %copy.59, bf16[4,96,256,1]{2,0,1,3:T(4,128)(2,1)S(1)} %copy-done.7), kind=kOutput, calls=%fused_computation.25 | convolution fusion | flops 382156800 | bytes 2146304 | tf_op jit(solution)/shard_map/kyqz,yhz->kyqh/dot_general | solution.py:67
  54.3 3.2 %copy.65 = bf16[20,4,96,96]{3,2,1,0:T(8,128)(2,1)S(1)} copy(bf16[20,4,96,96]{2,3,0,1:T(8,128)(2,1)} %convert_bitcast_fusion.1) | data formatting | bytes 2949120 | tf_op jit(solution)/shard_map/convert_element_type | solution.py:82
  57.5 0.0 copy-start.2
  57.5 0.0 copy-start.3
  57.6 3.6 %convert_element_type.97 = bf16[80,9216]{1,0:T(8,128)(2,1)} reshape(bf16[20,4,96,96]{3,2,1,0:T(8,128)(2,1)S(1)} %copy.65) | data formatting | bytes 2949120 | tf_op jit(solution)/shard_map/convert_element_type | solution.py:82
  61.1 0.0 all-reduce.3.cloned.1.call-update
  61.1 0.0 reduce-scatter.5.cloned.1.call-start
  61.2 0.6 gather_fusion.1
  61.8 0.6 gather_fusion
  62.3 0.1 broadcast_select_fusion
  62.4 0.1 broadcast_select_fusion.1
  62.5 0.1 broadcast_subtract_fusion
  62.6 0.2 sub.32
  62.8 2.3 tile.8
  65.0 4.3 %tile.9 = f32[80,9216]{1,0:T(8,128)} reshape(f32[20,4,9216]{2,1,0:T(4,128)} %tile.8) | data formatting | bytes 5898240 | tf_op jit(solution)/shard_map/tile | solution.py:39
  69.3 51.5 %all-reduce.3.cloned.1.call-done = bf16[80,9216]{1,0:T(8,128)(2,1)} async-done(((bf16[80,9216]{1,0:T(8,128)(2,1)}), bf16[80,9216]{1,0:T(8,128)(2,1)}) %all-reduce.3.cloned.1.call-update) | async-done | bytes 1474576 | tf_op jit(solution)/shard_map/psum | solution.py:82
  120.8 3.8 %multiply_convert_fusion.4 = bf16[80,9216]{1,0:T(8,128)(2,1)S(1)} fusion(f32[80,9216]{1,0:T(8,128)} %reshape.48, bf16[80,9216]{1,0:T(8,128)(2,1)} %all-reduce.3.cloned.1.call-done, f32[80,9216]{1,0:T(8,128)} %tile.9), kind=kLoop, calls=%fused_computation.21 | loop fusion | flops 5160960 | bytes 8847360 | tf_op jit(solution)/shard_map/convert_element_type | solution.py:78
  124.6 2.9 %reshape.46 = bf16[20,4,96,96]{3,2,1,0:T(8,128)(2,1)} reshape(bf16[80,9216]{1,0:T(8,128)(2,1)S(1)} %multiply_convert_fusion.4) | data formatting | bytes 2949120 | tf_op jit(solution)/shard_map/reshape | solution.py:43
  127.6 2.7 %fusion = bf16[20,4,256]{2,0,1:T(8,128)(2,1)S(1)} fusion(f32[4,96,256]{2,1,0:T(8,128)S(1)} %copy.59, bf16[20,4,96,96]{3,2,1,0:T(8,128)(2,1)} %reshape.46, bf16[4,96,256,1]{2,0,1,3:T(4,128)(2,1)S(1)} %copy-done.8), kind=kOutput, calls=%fused_computation.3 | convolution fusion | flops 381399040 | bytes 2105344 | tf_op jit(solution)/shard_map/iomx,oxj->iomj/dot_general | solution.py:44
  130.4 9.5 %all_gather.12 = bf16[80,2048]{1,0:T(8,128)(2,1)S(1)} all-gather(bf16[80,256]{1,0:T(8,128)(2,1)S(1)} %convert_element_type.102), channel_id=1, replica_groups=mesh['pb'=4,'row'=4,'col'=2] {'row','col'}, dimensions={1}, use_global_device_ids=true | all-gather | bytes 368640 | tf_op jit(solution)/shard_map/all_gather | solution.py:52
  139.8 1.1 convolution_convert_fusion.2
  140.9 0.0 reduce-scatter.5.cloned.1.call-update
  140.9 0.2 all-reduce.5.cloned.1.call-start
  141.2 7.4 %reduce-scatter.5.cloned.1.call-done = bf16[80,256]{1,0:T(8,128)(2,1)} async-done(((bf16[80,512]{1,0:T(8,128)(2,1)}), bf16[80,256]{1,0:T(8,128)(2,1)}) %reduce-scatter.5.cloned.1.call-update) | async-done | bytes 40976 | tf_op jit(solution)/shard_map/reduce_scatter | solution.py:58
  148.6 0.8 reshape.50
  149.4 2.9 %convert_bitcast_fusion = bf16[20,4,96,96]{2,3,0,1:T(8,128)(2,1)} fusion(f32[20,4,256]{2,0,1:T(8,128)S(1)} %copy.69, f32[4,96,256]{2,1,0:T(8,128)S(1)} %copy.59, bf16[4,96,256,1]{2,0,1,3:T(4,128)(2,1)S(1)} %copy-done.8), kind=kOutput, calls=%fused_computation.24 | convolution fusion | flops 382156800 | bytes 2146304 | tf_op jit(solution)/shard_map/kyqz,yhz->kyqh/dot_general | solution.py:67
  152.3 3.2 %copy.71 = bf16[20,4,96,96]{3,2,1,0:T(8,128)(2,1)S(1)} copy(bf16[20,4,96,96]{2,3,0,1:T(8,128)(2,1)} %convert_bitcast_fusion) | data formatting | bytes 2949120 | tf_op jit(solution)/shard_map/convert_element_type | solution.py:82
  155.5 3.6 %convert_element_type.107 = bf16[80,9216]{1,0:T(8,128)(2,1)} reshape(bf16[20,4,96,96]{3,2,1,0:T(8,128)(2,1)S(1)} %copy.71) | data formatting | bytes 2949120 | tf_op jit(solution)/shard_map/convert_element_type | solution.py:82
  159.1 0.0 all-reduce.5.cloned.1.call-update
  159.1 59.7 %all-reduce.5.cloned.1.call-done = bf16[80,9216]{1,0:T(8,128)(2,1)} async-done(((bf16[80,9216]{1,0:T(8,128)(2,1)}), bf16[80,9216]{1,0:T(8,128)(2,1)}) %all-reduce.5.cloned.1.call-update) | async-done | bytes 1474576 | tf_op jit(solution)/shard_map/psum | solution.py:82
  218.8 4.8 %fusion.12 = bf16[80,9216]{1,0:T(8,128)(2,1)S(1)} fusion(f32[80,9216]{1,0:T(8,128)} %reshape.48, f32[80,9216]{1,0:T(8,128)} %tile.9, bf16[80,9216]{1,0:T(8,128)(2,1)} %all-reduce.5.cloned.1.call-done, bf16[80,9216]{1,0:T(8,128)(2,1)} %all-reduce.3.cloned.1.call-done), kind=kLoop, calls=%fused_computation.20 | loop fusion | flops 11796480 | bytes 10321920 | tf_op jit(solution)/shard_map/convert_element_type | solution.py:79
  223.6 1.4 reshape.47
  (24 shorter events, 0.2 us)
Async XLA Ops:
  6.5 34.5 %copy-start = (bf16[1,512,1024]{2,1,0:T(8,128)(2,1)S(1)}, bf16[1,512,1024]{2,1,0:T(8,128)(2,1)}, u32[]{:S(2)}) copy-start(bf16[1,512,1024]{2,1,0:T(8,128)(2,1)} %param.15) | copy-start | bytes 3145732
  6.5 18.5 %copy-start.1 = (bf16[1,20,4,9216]{3,2,1,0:T(4,128)(2,1)S(1)}, bf16[1,20,4,9216]{3,2,1,0:T(4,128)(2,1)}, u32[]{:S(2)}) copy-start(bf16[1,20,4,9216]{3,2,1,0:T(4,128)(2,1)} %param.9) | copy-start | bytes 4423684
  6.5 44.1 %reduce-scatter.3.cloned.1.call-start = ((), (), s32[]{:S(2)}) async-start(), calls=%async_computation.2 | async-start | bytes 122880 | tf_op jit(solution)/shard_map/reduce_scatter | solution.py:58
  7.4 20.3 %copy-start.5 = (s32[4]{0:T(128)S(1)}, s32[4]{0:T(128)}, u32[]{:S(2)}) copy-start(s32[4]{0:T(128)} %param.11) | copy-start | bytes 52
  28.0 2.8 %copy-start.6 = (bf16[4,96,256,1]{2,0,1,3:T(4,128)(2,1)}, bf16[4,96,256,1]{2,0,1,3:T(4,128)(2,1)S(1)}, u32[]{:S(2)}) copy-start(bf16[4,96,256,1]{2,0,1,3:T(4,128)(2,1)S(1)} %fusion.16) | copy-start | bytes 589828
  41.0 2.9 %copy-start.4 = (s32[1,4,2]{1,2,0:T(2,128)S(1)}, s32[1,4,2]{1,2,0:T(2,128)}, u32[]{:S(2)}) copy-start(s32[1,4,2]{1,2,0:T(2,128)} %param.10) | copy-start | bytes 100
  42.1 9.3 %copy-start.7 = (bf16[4,96,256,1]{2,0,1,3:T(4,128)(2,1)S(1)}, bf16[4,96,256,1]{2,0,1,3:T(4,128)(2,1)}, u32[]{:S(2)}) copy-start(bf16[4,96,256,1]{2,0,1,3:T(4,128)(2,1)} %copy-done.6) | copy-start | bytes 589828
  42.1 78.7 %all-reduce.3.cloned.1.call-start = ((), (), s32[]{:S(2)}) async-start(), calls=%async_computation.3 | async-start | bytes 2949120 | tf_op jit(solution)/shard_map/psum | solution.py:82
  57.5 3.7 %copy-start.2 = (f32[4,96]{1,0:T(4,128)S(1)}, f32[4,96]{1,0:T(4,128)}, u32[]{:S(2)}) copy-start(f32[4,96]{1,0:T(4,128)} %param.13) | copy-start | bytes 4612
  57.5 4.2 %copy-start.3 = (f32[4,96]{1,0:T(4,128)S(1)}, f32[4,96]{1,0:T(4,128)}, u32[]{:S(2)}) copy-start(f32[4,96]{1,0:T(4,128)} %param.14) | copy-start | bytes 4612
  61.1 87.5 %reduce-scatter.5.cloned.1.call-start = ((), (), s32[]{:S(2)}) async-start(), calls=%async_computation.4 | async-start | bytes 122880 | tf_op jit(solution)/shard_map/reduce_scatter | solution.py:58
  124.6 2.9 %copy-start.8 = (bf16[4,96,256,1]{2,0,1,3:T(4,128)(2,1)S(1)}, bf16[4,96,256,1]{2,0,1,3:T(4,128)(2,1)}, u32[]{:S(2)}) copy-start(bf16[4,96,256,1]{2,0,1,3:T(4,128)(2,1)} %copy-done.6) | copy-start | bytes 589828
  140.9 77.9 %all-reduce.5.cloned.1.call-start = ((), (), s32[]{:S(2)}) async-start(), calls=%async_computation.5 | async-start | bytes 2949120 | tf_op jit(solution)/shard_map/psum | solution.py:82
Sparse Core Ops, SparseCore 0:
  42.2 8.3 reduce-scatter.2
  61.3 59.5 all-reduce.2
  141.1 7.5 reduce-scatter.4
  159.2 59.5 all-reduce.4
where the time goes:
time: 232 us
  waiting for transfers between devices  125 us (54%)
  blocking collectives  36.2 us (16%)
  local copies, waits for them, and re-layouts  32.7 us (14%)
  matrix products  14.8 us (6%)
  between operations  13.3 us (6%)
  other arithmetic  8.91 us (4%)
    psum x2, waiting for transfers between devices, finish(): lax.psum(partial_term.astype(jnp.bfloat16), ('row', 'col'))  111 us
    all_gather x2, blocking collectives, kernel_term(): everywhere = lax.all_gather(values, ('row', 'col'), axis=1, tiled=True)  19.6 us
    all_gather x1, blocking collectives, fetch_each(): found = pick(lax.all_gather(orbitals, 'pb', axis=0, tiled=True))  16.6 us
    reduce_scatter x2, waiting for transfers between devices, kernel_term(): lax.psum_scatter(partial_value.astype(jnp.bfloat16), 'col', scatter_dimen...  14.1 us
    convert_element_type x4, local copies, waits for them, and re-layouts, finish(): partial_term.astype(jnp.bfloat16)  13.5 us
    another operation x2, local copies, waits for them, and re-layouts, on_device(): gap_rows = jnp.tile(gap_grid, (vectors, 1))  6.56 us
    dot_general x2, matrix products, kernel_term(): jnp.einsum('kyqz,yhz->kyqh', weighted_product, conduction_orbital, prefer...  5.75 us
    dot_general x2, matrix products, kernel_term(): jnp.einsum('iomx,oxj->iomj', amplitude_lattice, conduction_orbital, prefe...  5.54 us
  transfers between devices with their start and end apart: 4, of which 4 were waited for; matrix products, arithmetic and copies ran while one was open for 4% of the time, Pallas kernels for 0%

commit v1 on v0

--- a/solution.py
+++ b/solution.py
@@ -49,7 +49,8 @@
         )
         values = jnp.sum(valence.astype(jnp.float32)[None] * inner_total_sum, axis=2)
         values = values.astype(jnp.bfloat16).reshape(vectors * pair_count, points)
-        everywhere = lax.all_gather(values, ("row", "col"), axis=1, tiled=True)
+        parts = lax.all_gather(values, ("row", "col"), axis=0, tiled=False)
+        everywhere = jnp.concatenate(parts, axis=1)
         needed = lax.dynamic_slice_in_dim(everywhere, column * col_width, col_width, 1)
         partial_value = lax.dot_general(
             needed, w_tile, (((1,), (1,)), ((), ())), preferred_element_type=jnp.float32

time: 232 us -> 231 us (level)
  no operation moved by 1% of the time
where the time goes in v1:
time: 231 us; the launch traced here: 230 us
  waiting for transfers between devices  126 us (55%)
  blocking collectives  35 us (15%)
  local copies, waits for them, and re-layouts  32.7 us (14%)
  matrix products  14.8 us (6%)
  between operations  13.4 us (6%)
  other arithmetic  8.91 us (4%)
    psum x2, waiting for transfers between devices, finish(): lax.psum(partial_term.astype(jnp.bfloat16), ('row', 'col'))  111 us
    all_gather x2, blocking collectives, kernel_term(): parts = lax.all_gather(values, ('row', 'col'), axis=0, tiled=False)  18.4 us
    all_gather x1, blocking collectives, fetch_each(): found = pick(lax.all_gather(orbitals, 'pb', axis=0, tiled=True))  16.6 us
    reduce_scatter x2, waiting for transfers between devices, kernel_term(): lax.psum_scatter(partial_value.astype(jnp.bfloat16), 'col', scatter_dimen...  14.4 us
    convert_element_type x4, local copies, waits for them, and re-layouts, finish(): partial_term.astype(jnp.bfloat16)  13.5 us
    another operation x2, local copies, waits for them, and re-layouts, on_device(): gap_rows = jnp.tile(gap_grid, (vectors, 1))  6.53 us
    dot_general x2, matrix products, kernel_term(): jnp.einsum('kyqz,yhz->kyqh', weighted_product, conduction_orbital, prefer...  5.75 us
    dot_general x2, matrix products, kernel_term(): jnp.einsum('iomx,oxj->iomj', amplitude_lattice, conduction_orbital, prefe...  5.54 us
  transfers between devices with their start and end apart: 4, of which 4 were waited for; matrix products, arithmetic and copies ran while one was open for 4% of the time, Pallas kernels for 0%

profile of v1, /device:TPU:0, one launch (start us, length us, event | category | flops | bytes accessed | tf_op | source)
XLA Modules:
  0.0 230.5 jit_solution(8881768181742684789)
XLA Ops:
  6.5 0.8 slice_bitcast_fusion.1
  7.4 16.6 %all_gather.10 = bf16[4,192,256]{2,1,0:T(8,128)(2,1)S(1)} all-gather(bf16[1,192,256]{2,1,0:T(8,128)(2,1)} %param.12), channel_id=1, replica_groups=mesh['pb'=4,'row'=4,'col'=2] {'pb'}, dimensions={0}, use_global_device_ids=true | all-gather | bytes 491520 | tf_op jit(solution)/shard_map/all_gather | solution.py:33
  24.0 1.0 fusion.15
  25.0 0.1 copy.62
  25.1 0.0 copy-done.1
  25.1 2.6 %reshape_reshape_squeeze.3 = bf16[20,4,96,96]{3,2,1,0:T(8,128)(2,1)} reshape(bf16[1,20,4,9216]{3,2,1,0:T(4,128)(2,1)S(1)} %copy-done.1) | data formatting | bytes 2949120 | tf_op jit(solution)/shard_map/reshape;reshape;squeeze | solution.py:43
  27.7 0.3 fusion.16
  28.0 2.8 %fusion.1 = bf16[20,4,256]{2,0,1:T(8,128)(2,1)S(1)} fusion(f32[4,96,256]{2,1,0:T(8,128)S(1)} %copy.62, bf16[20,4,96,96]{3,2,1,0:T(8,128)(2,1)} %reshape_reshape_squeeze.3, bf16[4,96,256,1]{2,0,1,3:T(4,128)(2,1)S(1)} %fusion.16), kind=kOutput, calls=%fused_computation.5 | convolution fusion | flops 381399040 | bytes 2105344 | tf_op jit(solution)/shard_map/iomx,oxj->iomj/dot_general | solution.py:44
  30.9 9.4 %all_gather.11 = bf16[8,80,256]{2,1,0:T(8,128)(2,1)S(1)} all-gather(bf16[1,80,256]{2,1,0:T(8,128)(2,1)S(1)} %convert_element_type.104), channel_id=1, replica_groups=mesh['pb'=4,'row'=4,'col'=2] {'row','col'}, dimensions={0}, use_global_device_ids=true | all-gather | bytes 368640 | tf_op jit(solution)/shard_map/all_gather | solution.py:52
  40.3 0.0 copy-start.4
  40.4 1.1 convolution_convert_fusion.3
  41.5 0.0 reduce-scatter.3.cloned.1.call-update
  41.5 0.0 all-reduce.3.cloned.1.call-start
  41.5 1.7 reshape.80
  43.3 6.7 %reduce-scatter.3.cloned.1.call-done = bf16[80,256]{1,0:T(8,128)(2,1)} async-done(((bf16[80,512]{1,0:T(8,128)(2,1)}), bf16[80,256]{1,0:T(8,128)(2,1)}) %reduce-scatter.3.cloned.1.call-update) | async-done | bytes 40976 | tf_op jit(solution)/shard_map/reduce_scatter | solution.py:59
  50.0 0.8 reshape.81
  50.8 2.9 %convert_bitcast_fusion.1 = bf16[20,4,96,96]{2,3,0,1:T(8,128)(2,1)} fusion(f32[20,4,256]{2,0,1:T(8,128)S(1)} %copy.67, f32[4,96,256]{2,1,0:T(8,128)S(1)} %copy.62, bf16[4,96,256,1]{2,0,1,3:T(4,128)(2,1)S(1)} %copy-done.7), kind=kOutput, calls=%fused_computation.25 | convolution fusion | flops 382156800 | bytes 2146304 | tf_op jit(solution)/shard_map/kyqz,yhz->kyqh/dot_general | solution.py:68
  53.7 3.2 %copy.69 = bf16[20,4,96,96]{3,2,1,0:T(8,128)(2,1)S(1)} copy(bf16[20,4,96,96]{2,3,0,1:T(8,128)(2,1)} %convert_bitcast_fusion.1) | data formatting | bytes 2949120 | tf_op jit(solution)/shard_map/convert_element_type | solution.py:83
  56.9 0.0 copy-start.2
  56.9 0.0 copy-start.3
  57.0 3.6 %convert_element_type.109 = bf16[80,9216]{1,0:T(8,128)(2,1)} reshape(bf16[20,4,96,96]{3,2,1,0:T(8,128)(2,1)S(1)} %copy.69) | data formatting | bytes 2949120 | tf_op jit(solution)/shard_map/convert_element_type | solution.py:83
  60.5 0.0 all-reduce.3.cloned.1.call-update
  60.5 0.0 reduce-scatter.5.cloned.1.call-start
  60.6 0.6 gather_fusion.1
  61.2 0.6 gather_fusion
  61.7 0.1 broadcast_select_fusion
  61.8 0.1 broadcast_select_fusion.1
  61.9 0.1 broadcast_subtract_fusion
  62.0 0.2 sub.32
  62.2 2.3 tile.8
  64.4 4.3 %tile.9 = f32[80,9216]{1,0:T(8,128)} reshape(f32[20,4,9216]{2,1,0:T(4,128)} %tile.8) | data formatting | bytes 5898240 | tf_op jit(solution)/shard_map/tile | solution.py:39
  68.7 51.5 %all-reduce.3.cloned.1.call-done = bf16[80,9216]{1,0:T(8,128)(2,1)} async-done(((bf16[80,9216]{1,0:T(8,128)(2,1)}), bf16[80,9216]{1,0:T(8,128)(2,1)}) %all-reduce.3.cloned.1.call-update) | async-done | bytes 1474576 | tf_op jit(solution)/shard_map/psum | solution.py:83
  120.2 3.8 %multiply_convert_fusion.4 = bf16[80,9216]{1,0:T(8,128)(2,1)S(1)} fusion(f32[80,9216]{1,0:T(8,128)} %reshape.80, bf16[80,9216]{1,0:T(8,128)(2,1)} %all-reduce.3.cloned.1.call-done, f32[80,9216]{1,0:T(8,128)} %tile.9), kind=kLoop, calls=%fused_computation.21 | loop fusion | flops 5160960 | bytes 8847360 | tf_op jit(solution)/shard_map/convert_element_type | solution.py:79
  124.0 2.9 %reshape.76 = bf16[20,4,96,96]{3,2,1,0:T(8,128)(2,1)} reshape(bf16[80,9216]{1,0:T(8,128)(2,1)S(1)} %multiply_convert_fusion.4) | data formatting | bytes 2949120 | tf_op jit(solution)/shard_map/reshape | solution.py:43
  126.9 2.7 %fusion = bf16[20,4,256]{2,0,1:T(8,128)(2,1)S(1)} fusion(f32[4,96,256]{2,1,0:T(8,128)S(1)} %copy.62, bf16[20,4,96,96]{3,2,1,0:T(8,128)(2,1)} %reshape.76, bf16[4,96,256,1]{2,0,1,3:T(4,128)(2,1)S(1)} %copy-done.8), kind=kOutput, calls=%fused_computation.3 | convolution fusion | flops 381399040 | bytes 2105344 | tf_op jit(solution)/shard_map/iomx,oxj->iomj/dot_general | solution.py:44
  129.7 9.0 %all_gather.12 = bf16[8,80,256]{2,1,0:T(8,128)(2,1)S(1)} all-gather(bf16[1,80,256]{2,1,0:T(8,128)(2,1)S(1)} %convert_element_type.114), channel_id=1, replica_groups=mesh['pb'=4,'row'=4,'col'=2] {'row','col'}, dimensions={0}, use_global_device_ids=true | all-gather | bytes 368640 | tf_op jit(solution)/shard_map/all_gather | solution.py:52
  138.7 1.1 convolution_convert_fusion.2
  139.8 0.0 reduce-scatter.5.cloned.1.call-update
  139.8 0.0 all-reduce.5.cloned.1.call-start
  139.9 7.6 %reduce-scatter.5.cloned.1.call-done = bf16[80,256]{1,0:T(8,128)(2,1)} async-done(((bf16[80,512]{1,0:T(8,128)(2,1)}), bf16[80,256]{1,0:T(8,128)(2,1)}) %reduce-scatter.5.cloned.1.call-update) | async-done | bytes 40976 | tf_op jit(solution)/shard_map/reduce_scatter | solution.py:59
  147.5 0.8 reshape.82
  148.4 2.9 %convert_bitcast_fusion = bf16[20,4,96,96]{2,3,0,1:T(8,128)(2,1)} fusion(f32[20,4,256]{2,0,1:T(8,128)S(1)} %copy.74, f32[4,96,256]{2,1,0:T(8,128)S(1)} %copy.62, bf16[4,96,256,1]{2,0,1,3:T(4,128)(2,1)S(1)} %copy-done.8), kind=kOutput, calls=%fused_computation.24 | convolution fusion | flops 382156800 | bytes 2146304 | tf_op jit(solution)/shard_map/kyqz,yhz->kyqh/dot_general | solution.py:68
  151.2 3.2 %copy.76 = bf16[20,4,96,96]{3,2,1,0:T(8,128)(2,1)S(1)} copy(bf16[20,4,96,96]{2,3,0,1:T(8,128)(2,1)} %convert_bitcast_fusion) | data formatting | bytes 2949120 | tf_op jit(solution)/shard_map/convert_element_type | solution.py:83
  154.4 3.6 %convert_element_type.119 = bf16[80,9216]{1,0:T(8,128)(2,1)} reshape(bf16[20,4,96,96]{3,2,1,0:T(8,128)(2,1)S(1)} %copy.76) | data formatting | bytes 2949120 | tf_op jit(solution)/shard_map/convert_element_type | solution.py:83
  158.0 0.0 all-reduce.5.cloned.1.call-update
  158.0 59.7 %all-reduce.5.cloned.1.call-done = bf16[80,9216]{1,0:T(8,128)(2,1)} async-done(((bf16[80,9216]{1,0:T(8,128)(2,1)}), bf16[80,9216]{1,0:T(8,128)(2,1)}) %all-reduce.5.cloned.1.call-update) | async-done | bytes 1474576 | tf_op jit(solution)/shard_map/psum | solution.py:83
  217.7 4.8 %fusion.12 = bf16[80,9216]{1,0:T(8,128)(2,1)S(1)} fusion(f32[80,9216]{1,0:T(8,128)} %reshape.80, f32[80,9216]{1,0:T(8,128)} %tile.9, bf16[80,9216]{1,0:T(8,128)(2,1)} %all-reduce.5.cloned.1.call-done, bf16[80,9216]{1,0:T(8,128)(2,1)} %all-reduce.3.cloned.1.call-done), kind=kLoop, calls=%fused_computation.20 | loop fusion | flops 11796480 | bytes 10321920 | tf_op jit(solution)/shard_map/convert_element_type | solution.py:80
  222.5 1.4 reshape.79
  (26 shorter events, 0.2 us)
Async XLA Ops:
  6.5 33.8 %copy-start = (bf16[1,512,1024]{2,1,0:T(8,128)(2,1)S(1)}, bf16[1,512,1024]{2,1,0:T(8,128)(2,1)}, u32[]{:S(2)}) copy-start(bf16[1,512,1024]{2,1,0:T(8,128)(2,1)} %param.15) | copy-start | bytes 3145732
  6.5 18.5 %copy-start.1 = (bf16[1,20,4,9216]{3,2,1,0:T(4,128)(2,1)S(1)}, bf16[1,20,4,9216]{3,2,1,0:T(4,128)(2,1)}, u32[]{:S(2)}) copy-start(bf16[1,20,4,9216]{3,2,1,0:T(4,128)(2,1)} %param.9) | copy-start | bytes 4423684
  6.5 43.5 %reduce-scatter.3.cloned.1.call-start = ((), (), s32[]{:S(2)}) async-start(), calls=%async_computation.2 | async-start | bytes 122880 | tf_op jit(solution)/shard_map/reduce_scatter | solution.py:59
  7.4 20.3 %copy-start.5 = (s32[4]{0:T(128)S(1)}, s32[4]{0:T(128)}, u32[]{:S(2)}) copy-start(s32[4]{0:T(128)} %param.11) | copy-start | bytes 52
  28.0 2.9 %copy-start.6 = (bf16[4,96,256,1]{2,0,1,3:T(4,128)(2,1)}, bf16[4,96,256,1]{2,0,1,3:T(4,128)(2,1)S(1)}, u32[]{:S(2)}) copy-start(bf16[4,96,256,1]{2,0,1,3:T(4,128)(2,1)S(1)} %fusion.16) | copy-start | bytes 589828
  40.3 2.9 %copy-start.4 = (s32[1,4,2]{1,2,0:T(2,128)S(1)}, s32[1,4,2]{1,2,0:T(2,128)}, u32[]{:S(2)}) copy-start(s32[1,4,2]{1,2,0:T(2,128)} %param.10) | copy-start | bytes 100
  41.5 9.4 %copy-start.7 = (bf16[4,96,256,1]{2,0,1,3:T(4,128)(2,1)S(1)}, bf16[4,96,256,1]{2,0,1,3:T(4,128)(2,1)}, u32[]{:S(2)}) copy-start(bf16[4,96,256,1]{2,0,1,3:T(4,128)(2,1)} %copy-done.6) | copy-start | bytes 589828
  41.5 78.7 %all-reduce.3.cloned.1.call-start = ((), (), s32[]{:S(2)}) async-start(), calls=%async_computation.3 | async-start | bytes 2949120 | tf_op jit(solution)/shard_map/psum | solution.py:83
  56.9 3.7 %copy-start.2 = (f32[4,96]{1,0:T(4,128)S(1)}, f32[4,96]{1,0:T(4,128)}, u32[]{:S(2)}) copy-start(f32[4,96]{1,0:T(4,128)} %param.13) | copy-start | bytes 4612
  56.9 4.2 %copy-start.3 = (f32[4,96]{1,0:T(4,128)S(1)}, f32[4,96]{1,0:T(4,128)}, u32[]{:S(2)}) copy-start(f32[4,96]{1,0:T(4,128)} %param.14) | copy-start | bytes 4612
  60.5 87.0 %reduce-scatter.5.cloned.1.call-start = ((), (), s32[]{:S(2)}) async-start(), calls=%async_computation.4 | async-start | bytes 122880 | tf_op jit(solution)/shard_map/reduce_scatter | solution.py:59
  124.0 2.9 %copy-start.8 = (bf16[4,96,256,1]{2,0,1,3:T(4,128)(2,1)S(1)}, bf16[4,96,256,1]{2,0,1,3:T(4,128)(2,1)}, u32[]{:S(2)}) copy-start(bf16[4,96,256,1]{2,0,1,3:T(4,128)(2,1)} %copy-done.6) | copy-start | bytes 589828
  139.8 77.8 %all-reduce.5.cloned.1.call-start = ((), (), s32[]{:S(2)}) async-start(), calls=%async_computation.5 | async-start | bytes 2949120 | tf_op jit(solution)/shard_map/psum | solution.py:83
Sparse Core Ops, SparseCore 0:
  41.6 8.3 reduce-scatter.2
  60.7 59.5 all-reduce.2
  140.0 7.5 reduce-scatter.4
  158.1 59.5 all-reduce.4
